TPU v7x, 512 devices: a whole 4x4x16 slice. The times are simulated.
512 devices in a mesh: dp: 32 (over z, core), tensor: 16 (over y, x).
Axes of the slice: x: 4, y: 4, z: 16, core: 2. Of those that a mesh axis runs over, the one named last changes fastest.
Arguments:
- dout: bfloat16 [12288, 5120], P(('dp', 'tensor')), may hold values from -0.75 to 0.75
- attn_ctx: bfloat16 [12288, 5120], P('dp', 'tensor'), may hold values from -6 to 6
- mlp_hidden: bfloat16 [12288, 13824], P('dp', 'tensor'), may hold values from -6 to 6
- w_out: bfloat16 [5120, 5120], P('tensor', 'dp'), may hold values from -0.078125 to 0.078125
- w_down: bfloat16 [13824, 5120], P('tensor', 'dp'), may hold values from -0.0546875 to 0.0546875
- head_logits: float32 [40], replicated, may hold values from -2 to 3
- unit_logits: float32 [13824], P('tensor'), may hold values from -2 to 3
- head_noise: float32 [40], replicated, may hold values from 0.001 to 0.999
- unit_noise: float32 [13824], P('tensor'), may hold values from 0.001 to 0.999
- linear_mult: float32 [1], replicated, may hold values from 100 to 300
- square_mult: float32 [1], replicated, may hold values from 1 to 4
- target: float32 [1], replicated, may hold values from 40 to 70
Outputs:
- ctx_grad: bfloat16 [12288, 5120], P('dp', 'tensor')
- hidden_grad: bfloat16 [12288, 13824], P('dp', 'tensor')
- head_grad: float32 [40], replicated
- unit_grad: float32 [13824], P('tensor')
All inputs are finite; a program needn't handle non-finite values.
Results may differ from a plain program's by a relative error of at most 0.001.
Values may be sent and summed in bfloat16 or wider, within the bound.
No kernel may reach another device: no remote copies, remote signals or barrier semaphores. Data moves between devices by JAX's collectives and lax.ppermute only.
A program may use at most 64 MiB of HBM per device.

v0:
```python
import jax
import jax.numpy as jnp
from jax import lax
from jax.sharding import PartitionSpec as P

H = 40
HEAD = 128
FF = 13824
low_end = -0.1
high_end = 1.1
temper = 2.0 / 3.0


def concrete(logits, noise):
    shape_s = jax.nn.sigmoid((jnp.log(noise) - jnp.log(1.0 - noise) + logits) / temper)
    stretched = shape_s * (high_end - low_end) + low_end
    gate = jnp.clip(stretched, 0.0, 1.0)
    inside = jnp.logical_and(stretched > 0.0, stretched < 1.0)
    slope = jnp.where(
        inside, (high_end - low_end) / temper * shape_s * (1.0 - shape_s), 0.0 * shape_s
    )
    return (gate, slope)


def open_prob(logits):
    return jax.nn.sigmoid(logits - temper * jnp.log(-low_end / high_end))


def local(
    dout,
    attn_ctx,
    mlp_hidden,
    w_out,
    w_down,
    head_logits,
    unit_logits,
    head_noise,
    unit_noise,
    linear_mult,
    square_mult,
    target,
):
    head_gate, head_slope = concrete(head_logits, head_noise)
    unit_gate, unit_slope = concrete(unit_logits, unit_noise)
    col_count = attn_ctx.shape[1]
    head_total = head_logits.shape[0]
    tensor_index = lax.axis_index("tensor")
    columns = tensor_index * col_count + lax.iota(jnp.int32, col_count)
    owner = columns // HEAD
    member = (owner[:, None] == lax.iota(jnp.int32, head_total)[None, :]).astype(jnp.float32)
    col_gate = jnp.dot(member, head_gate, precision=lax.Precision.HIGHEST)
    full_rows = lax.all_gather(dout, "tensor", axis=0, tiled=True)
    dims = (((1,), (1,)), ((), ()))

    def contract(piece):
        return lax.dot_general(full_rows, piece, dims, preferred_element_type=jnp.float32)

    ctx_pre = contract(lax.all_gather(w_out, "dp", axis=1, tiled=True))
    hid_pre = contract(lax.all_gather(w_down, "dp", axis=1, tiled=True))
    ctx_grad = (ctx_pre * col_gate[None, :]).astype(jnp.bfloat16)
    hidden_grad = (hid_pre * unit_gate[None, :]).astype(jnp.bfloat16)
    col_part = jnp.sum(attn_ctx.astype(jnp.float32) * ctx_pre, axis=0)
    unit_part = jnp.sum(mlp_hidden.astype(jnp.float32) * hid_pre, axis=0)
    head_part = jnp.dot(col_part, member, precision=lax.Precision.HIGHEST)
    p_head = open_prob(head_logits)
    p_unit = open_prob(unit_logits)
    local_mass = jnp.sum(p_unit)
    unit_data = lax.psum(unit_part, "dp")
    head_data = lax.psum(head_part, ("dp", "tensor"))
    unit_mass = lax.psum(local_mass, "tensor")
    denom = 4.0 * HEAD * H + 3.0 * FF
    size = 100.0 * (4.0 * HEAD * jnp.sum(p_head) + 3.0 * unit_mass) / denom
    factor = linear_mult[0] + 2.0 * square_mult[0] * (size - target[0])
    head_grad = head_data * head_slope + factor * (400.0 * HEAD / denom) * p_head * (1.0 - p_head)
    unit_grad = unit_data * unit_slope + factor * (300.0 / denom) * p_unit * (1.0 - p_unit)
    return (ctx_grad, hidden_grad, head_grad, unit_grad)


def solution(mesh):
    placed = (
        P(("dp", "tensor"), None),
        P("dp", "tensor"),
        P("dp", "tensor"),
        P("tensor", "dp"),
        P("tensor", "dp"),
        P(),
        P("tensor"),
        P(),
        P("tensor"),
        P(),
        P(),
        P(),
    )
    return jax.shard_map(
        local,
        mesh=mesh,
        in_specs=placed,
        out_specs=(P("dp", "tensor"), P("dp", "tensor"), P(), P("tensor")),
        check_vma=False,
    )
```

profile of v0, /device:TPU:1, one launch (start us, length us, event | category | flops | bytes accessed | tf_op | source)
XLA Modules:
  0.0 329.6 jit_solution(5489138382124432926)
XLA Ops:
  7.2 0.0 all-gather.6.cloned.1.call-start
  7.2 0.7 all-gather.6.cloned.1.call-update
  7.9 0.0 all-gather.4.cloned.1.call-start
  7.9 0.7 all-gather.4.cloned.1.call-update
  8.6 0.0 all-gather.8.cloned.1.call-start
  8.7 0.7 all-gather.8.cloned.1.call-update
  9.4 1.3 fusion.2
  10.7 34.9 %psum.22 = f32[]{:T(128)} all-reduce(f32[]{:T(128)} %get-tuple-element.11), channel_id=1, replica_groups=mesh['dp'=32,'tensor'=16] {'tensor'}, use_global_device_ids=true, to_apply=%region_4.5 | all-reduce | flops 1 | bytes 8 | tf_op jit(solution)/shard_map/psum | solution.py:70
  48.2 1.3 fusion.17
  50.1 0.0 copy-start.2
  50.1 0.0 copy-start.3
  50.2 0.0 copy-start.4
  50.2 38.7 %all-gather.6.cloned.1.call-done = bf16[320,5120]{0,1:T(8,128)(2,1)} async-done(((bf16[320,160]{0,1:T(8,128)(2,1)}), bf16[320,5120]{0,1:T(8,128)(2,1)}) %all-gather.6.cloned.1.call-update) | async-done | bytes 3276816 | tf_op jit(solution)/shard_map/all_gather | solution.py:58
  88.8 65.0 %all-gather.4.cloned.1.call-done = bf16[384,5120]{1,0:T(8,128)(2,1)} async-done(((bf16[24,5120]{1,0:T(8,128)(2,1)}), bf16[384,5120]{1,0:T(8,128)(2,1)}) %all-gather.4.cloned.1.call-update) | async-done | bytes 3932176 | tf_op jit(solution)/shard_map/all_gather | solution.py:52
  153.9 5.3 %multiply_reduce_fusion.1 = (f32[320]{0:T(512)S(1)}, f32[384,320]{0,1:T(8,128)S(1)}) fusion(bf16[384,320]{0,1:T(8,128)(2,1)} %param.13, bf16[384,5120]{1,0:T(8,128)(2,1)} %all-gather.4.cloned.1.call-done, bf16[320,5120]{0,1:T(8,128)(2,1)} %all-gather.6.cloned.1.call-done), kind=kOutput, calls=%fused_computation.4 | convolution fusion | flops 1258659584 | bytes 7947520 | tf_op jit(solution)/shard_map/dot_general | solution.py:56
  159.2 0.2 convolution_bitcast_fusion
  159.5 105.0 %psum.21 = f32[40]{0:T(128)S(1)} all-reduce(f32[40]{0:T(128)S(1)} %convolution_bitcast_fusion), channel_id=1, replica_groups=mesh['dp'=32,'tensor'=16] {'dp','tensor'}, use_global_device_ids=true, to_apply=%region_1.2 | all-reduce | flops 40 | bytes 320 | tf_op jit(solution)/shard_map/psum | solution.py:69
  264.5 0.0 copy-done.2
  264.5 0.0 copy-done.3
  264.5 0.5 multiply_add_fusion.2
  265.0 0.3 convolution_reduce_fusion
  265.3 0.8 multiply_convert_fusion.1
  266.1 0.0 all-gather.8.cloned.1.call-done
  266.2 0.0 copy-done.4
  266.2 0.0 copy-start
  266.2 0.0 copy-start.1
  266.2 10.5 %multiply_reduce_fusion = (f32[864]{0:T(1024)S(1)}, bf16[384,864]{0,1:T(8,128)(2,1)}) fusion(bf16[384,864]{0,1:T(8,128)(2,1)S(1)} %copy-done.4, f32[864]{0:T(1024)S(1)} %get-tuple-element.10, bf16[384,5120]{1,0:T(8,128)(2,1)} %all-gather.4.cloned.1.call-done, bf16[864,5120]{0,1:T(8,128)(2,1)} %all-gather.8.cloned.1.call-done), kind=kOutput, calls=%fused_computation | convolution fusion | flops 3399044352 | bytes 14113536 | tf_op jit(solution)/shard_map/dot_general | solution.py:56
  276.7 45.8 %psum.23 = f32[864]{0:T(1024)S(1)} all-reduce(f32[864]{0:T(1024)S(1)} %get-tuple-element.8), channel_id=1, replica_groups=mesh['dp'=32,'tensor'=16] {'dp'}, use_global_device_ids=true, to_apply=%region_6.7 | all-reduce | flops 864 | bytes 6912 | tf_op jit(solution)/shard_map/psum | solution.py:68
  322.5 0.0 copy-done
  322.5 0.0 copy-done.1
  322.5 0.6 multiply_add_fusion
  (2 shorter events, 0.0 us)
Async XLA Ops:
  7.2 81.7 %all-gather.6.cloned.1.call-start = ((), (), s32[]{:S(2)}) async-start(), calls=%async_computation.1 | async-start | bytes 4055040 | tf_op jit(solution)/shard_map/all_gather | solution.py:58
  7.9 146.0 %all-gather.4.cloned.1.call-start = ((), (), s32[]{:S(2)}) async-start(), calls=%async_computation | async-start | bytes 4177920 | tf_op jit(solution)/shard_map/all_gather | solution.py:52
  8.6 257.5 %all-gather.8.cloned.1.call-start = ((), (), s32[]{:S(2)}) async-start(), calls=%async_computation.2 | async-start | bytes 9461760 | tf_op jit(solution)/shard_map/all_gather | solution.py:59
  50.1 214.4 %copy-start.2 = (f32[40]{0:T(128)S(1)}, f32[40]{0:T(128)}, u32[]{:S(2)}) copy-start(f32[40]{0:T(128)} %param.17) | copy-start | bytes 484
  50.1 214.4 %copy-start.3 = (f32[40]{0:T(128)S(1)}, f32[40]{0:T(128)}, u32[]{:S(2)}) copy-start(f32[40]{0:T(128)} %param.19) | copy-start | bytes 484
  50.2 216.0 %copy-start.4 = (bf16[384,864]{0,1:T(8,128)(2,1)S(1)}, bf16[384,864]{0,1:T(8,128)(2,1)}, u32[]{:S(2)}) copy-start(bf16[384,864]{0,1:T(8,128)(2,1)} %param.14) | copy-start | bytes 1990660
  266.2 56.3 %copy-start = (f32[864]{0:T(1024)S(1)}, f32[864]{0:T(1024)}, u32[]{:S(2)}) copy-start(f32[864]{0:T(1024)} %param.18) | copy-start | bytes 10372
  266.2 56.3 %copy-start.1 = (f32[864]{0:T(1024)S(1)}, f32[864]{0:T(1024)}, u32[]{:S(2)}) copy-start(f32[864]{0:T(1024)} %param.20) | copy-start | bytes 10372
Sparse Core Ops, SparseCore 0:
  10.1 78.6 all-gather.5
  91.8 61.9 all-gather.3
  156.0 80.5 all-gather.7
where the time goes:
time: 330 us
  blocking collectives  186 us (56%)
  waiting for transfers between devices  106 us (32%)
  between operations  17.1 us (5%)
  matrix products  16.4 us (5%)
  other arithmetic  4.6 us (1%)
    psum x1, blocking collectives, local(): head_data = lax.psum(head_part, ('dp', 'tensor'))  105 us
    all_gather x1, waiting for transfers between devices, local(): full_rows = lax.all_gather(dout, 'tensor', axis=0, tiled=True)  65 us
    psum x1, blocking collectives, local(): unit_data = lax.psum(unit_part, 'dp')  45.8 us
    all_gather x1, waiting for transfers between devices, local(): ctx_pre = contract(lax.all_gather(w_out, 'dp', axis=1, tiled=True))  38.7 us
    psum x1, blocking collectives, local(): unit_mass = lax.psum(local_mass, 'tensor')  34.9 us
    dot_general x2, matrix products, contract(): lax.dot_general(full_rows, piece, dims, preferred_element_type=jnp.float32)  15.9 us
  transfers between devices with their start and end apart: 3, of which 2 were waited for; matrix products, arithmetic and copies ran while one was open for 3% of the time, Pallas kernels for 0%

commit v1 on v0

--- a/solution.py
+++ b/solution.py
@@ -66,7 +66,7 @@
     p_unit = open_prob(unit_logits)
     local_mass = jnp.sum(p_unit)
     unit_data = lax.psum(unit_part, "dp")
-    head_data = lax.psum(head_part, ("dp", "tensor"))
+    head_data = lax.psum(lax.psum(head_part, "tensor"), "dp")
     unit_mass = lax.psum(local_mass, "tensor")
     denom = 4.0 * HEAD * H + 3.0 * FF
     size = 100.0 * (4.0 * HEAD * jnp.sum(p_head) + 3.0 * unit_mass) / denom

time: 330 us -> 303 us (0.918)
  blocking collectives: 186 us -> 78.2 us
  waiting for transfers between devices: 106 us -> 185 us
    psum x3 -> x2, blocking collectives: 186 us -> 78.2 us  [local(): head_data = lax.psum(lax.psum(head_part, 'tensor'), 'dp')]
    all_gather x1, waiting for transfers between devices: 0.01 us -> 43.7 us  [local(): hid_pre = contract(lax.all_gather(w_down, 'dp', axis=1, tiled=True))]
    all_gather x1, waiting for transfers between devices: 38.7 us -> 74.3 us  [local(): ctx_pre = contract(lax.all_gather(w_out, 'dp', axis=1, tiled=True))]
  transfers between devices with their start and end apart: 3 -> 3, of which waited for: 2 -> 3; matrix products, arithmetic and copies ran while one was open for 3% -> 3% of each run, Pallas kernels for 0% -> 0%
where the time goes in v1:
time: 303 us; the launch traced here: 301 us
  waiting for transfers between devices  185 us (61%)
  blocking collectives  78.2 us (26%)
  between operations  17.1 us (6%)
  matrix products  16.4 us (5%)
  other arithmetic  4.6 us (2%)
    psum x2, blocking collectives, local(): head_data = lax.psum(lax.psum(head_part, 'tensor'), 'dp')  78.2 us
    all_gather x1, waiting for transfers between devices, local(): ctx_pre = contract(lax.all_gather(w_out, 'dp', axis=1, tiled=True))  74.3 us
    all_gather x1, waiting for transfers between devices, local(): full_rows = lax.all_gather(dout, 'tensor', axis=0, tiled=True)  64.8 us
    all_gather x1, waiting for transfers between devices, local(): hid_pre = contract(lax.all_gather(w_down, 'dp', axis=1, tiled=True))  43.7 us
    dot_general x2, matrix products, contract(): lax.dot_general(full_rows, piece, dims, preferred_element_type=jnp.float32)  15.9 us
  transfers between devices with their start and end apart: 3, of which 3 were waited for; matrix products, arithmetic and copies ran while one was open for 3% of the time, Pallas kernels for 0%

profile of v1, /device:TPU:1, one launch (start us, length us, event | category | flops | bytes accessed | tf_op | source)
XLA Modules:
  0.0 301.3 jit_solution(986423120768863830)
XLA Ops:
  7.2 0.0 all-gather.6.cloned.1.call-start
  7.2 0.7 all-gather.6.cloned.1.call-update
  7.9 0.0 all-gather.4.cloned.1.call-start
  7.9 0.7 all-gather.4.cloned.1.call-update
  8.6 0.0 all-gather.8.cloned.1.call-start
  8.7 0.7 all-gather.8.cloned.1.call-update
  11.3 1.3 fusion.17
  13.3 1.3 fusion.2
  14.6 0.0 copy-start.4
  14.6 74.3 %all-gather.6.cloned.1.call-done = bf16[320,5120]{0,1:T(8,128)(2,1)} async-done(((bf16[320,160]{0,1:T(8,128)(2,1)}), bf16[320,5120]{0,1:T(8,128)(2,1)}) %all-gather.6.cloned.1.call-update) | async-done | bytes 3276816 | tf_op jit(solution)/shard_map/all_gather | solution.py:58
  88.9 64.8 %all-gather.4.cloned.1.call-done = bf16[384,5120]{1,0:T(8,128)(2,1)} async-done(((bf16[24,5120]{1,0:T(8,128)(2,1)}), bf16[384,5120]{1,0:T(8,128)(2,1)}) %all-gather.4.cloned.1.call-update) | async-done | bytes 3932176 | tf_op jit(solution)/shard_map/all_gather | solution.py:52
  153.7 5.3 %multiply_reduce_fusion.1 = (f32[320]{0:T(512)S(1)}, f32[384,320]{0,1:T(8,128)S(1)}) fusion(bf16[384,320]{0,1:T(8,128)(2,1)} %param.13, bf16[384,5120]{1,0:T(8,128)(2,1)} %all-gather.4.cloned.1.call-done, bf16[320,5120]{0,1:T(8,128)(2,1)} %all-gather.6.cloned.1.call-done), kind=kOutput, calls=%fused_computation.4 | convolution fusion | flops 1258659584 | bytes 7947520 | tf_op jit(solution)/shard_map/dot_general | solution.py:56
  159.1 0.2 convolution_bitcast_fusion
  159.3 31.8 %all-reduce.1 = (f32[40]{0:T(128)S(1)}, f32[]{:T(128)}) all-reduce(f32[40]{0:T(128)S(1)} %convolution_bitcast_fusion, f32[]{:T(128)} %get-tuple-element.15), channel_id=1, replica_groups=mesh['dp'=32,'tensor'=16] {'tensor'}, use_global_device_ids=true, to_apply=%region_1.2 | all-reduce | flops 41 | bytes 328 | tf_op jit(solution)/shard_map/psum | solution.py:69
  191.8 43.7 %all-gather.8.cloned.1.call-done = bf16[864,5120]{0,1:T(8,128)(2,1)} async-done(((bf16[864,160]{0,1:T(8,128)(2,1)}), bf16[864,5120]{0,1:T(8,128)(2,1)}) %all-gather.8.cloned.1.call-update) | async-done | bytes 8847376 | tf_op jit(solution)/shard_map/all_gather | solution.py:59
  235.5 0.0 copy-done.4
  235.5 0.0 copy-start.2
  235.5 0.0 copy-start.3
  235.5 0.0 copy-start
  235.5 0.0 copy-start.1
  235.5 10.5 %multiply_convert_fusion = (bf16[384,864]{0,1:T(8,128)(2,1)}, f32[864]{0:T(1024)S(1)}) fusion(f32[864]{0:T(1024)S(1)} %get-tuple-element.14, bf16[384,864]{0,1:T(8,128)(2,1)S(1)} %copy-done.4, bf16[384,5120]{1,0:T(8,128)(2,1)} %all-gather.4.cloned.1.call-done, bf16[864,5120]{0,1:T(8,128)(2,1)} %all-gather.8.cloned.1.call-done), kind=kOutput, calls=%fused_computation.1 | convolution fusion | flops 3399044352 | bytes 14113536 | tf_op jit(solution)/shard_map/dot_general | solution.py:56
  246.1 46.4 %all-reduce = (f32[40]{0:T(128)S(1)}, f32[864]{0:T(1024)S(1)}) all-reduce(f32[40]{0:T(128)S(1)} %get-tuple-element.6, f32[864]{0:T(1024)S(1)} %get-tuple-element.13), channel_id=1, replica_groups=mesh['dp'=32,'tensor'=16] {'dp'}, use_global_device_ids=true, to_apply=%region_2.3 | all-reduce | flops 904 | bytes 7232 | tf_op jit(solution)/shard_map/psum | solution.py:69
  292.4 0.0 copy-done.2
  292.4 0.0 copy-done.3
  292.5 0.5 multiply_add_fusion.2
  293.0 0.3 convolution_reduce_fusion
  293.3 0.8 multiply_convert_fusion.1
  294.1 0.0 copy-done
  294.1 0.0 copy-done.1
  294.1 0.6 multiply_add_fusion
  (2 shorter events, 0.0 us)
Async XLA Ops:
  7.2 81.8 %all-gather.6.cloned.1.call-start = ((), (), s32[]{:S(2)}) async-start(), calls=%async_computation.1 | async-start | bytes 4055040 | tf_op jit(solution)/shard_map/all_gather | solution.py:58
  7.9 145.8 %all-gather.4.cloned.1.call-start = ((), (), s32[]{:S(2)}) async-start(), calls=%async_computation | async-start | bytes 4177920 | tf_op jit(solution)/shard_map/all_gather | solution.py:52
  8.6 226.9 %all-gather.8.cloned.1.call-start = ((), (), s32[]{:S(2)}) async-start(), calls=%async_computation.2 | async-start | bytes 9461760 | tf_op jit(solution)/shard_map/all_gather | solution.py:59
  14.6 220.9 %copy-start.4 = (bf16[384,864]{0,1:T(8,128)(2,1)S(1)}, bf16[384,864]{0,1:T(8,128)(2,1)}, u32[]{:S(2)}) copy-start(bf16[384,864]{0,1:T(8,128)(2,1)} %param.14) | copy-start | bytes 1990660
  235.5 56.9 %copy-start.2 = (f32[40]{0:T(128)S(1)}, f32[40]{0:T(128)}, u32[]{:S(2)}) copy-start(f32[40]{0:T(128)} %param.17) | copy-start | bytes 484
  235.5 56.9 %copy-start.3 = (f32[40]{0:T(128)S(1)}, f32[40]{0:T(128)}, u32[]{:S(2)}) copy-start(f32[40]{0:T(128)} %param.19) | copy-start | bytes 484
  235.5 58.6 %copy-start = (f32[864]{0:T(1024)S(1)}, f32[864]{0:T(1024)}, u32[]{:S(2)}) copy-start(f32[864]{0:T(1024)} %param.18) | copy-start | bytes 10372
  235.5 58.6 %copy-start.1 = (f32[864]{0:T(1024)S(1)}, f32[864]{0:T(1024)}, u32[]{:S(2)}) copy-start(f32[864]{0:T(1024)} %param.20) | copy-start | bytes 10372
Sparse Core Ops, SparseCore 0:
  10.1 78.7 all-gather.5
  91.9 61.7 all-gather.3
  155.9 79.6 all-gather.7
